TPU v7x, 512 devices: a whole 4x8x8 slice. The times are simulated.
512 devices in a mesh: seq: 64 (over z, x, y_lo), tp: 8 (over y_hi, core).
Axes of the slice: x: 4, y: 8 (y_hi: 4, y_lo: 2; y = y_hi * 2 + y_lo), z: 8, core: 2. Of those that a mesh axis runs over, the one named last changes fastest.
Arguments:
- tokens: bfloat16 [16384, 4096], P('seq', 'tp'), may hold values from -6 to 6
- x_weight: bfloat16 [4096, 8192], P('seq', 'tp'), may hold values from -0.09375 to 0.09375
- bc_weight: bfloat16 [4096, 256], P('seq', 'tp'), may hold values from -0.09375 to 0.09375
- dt_weight: bfloat16 [4096, 128], P('seq', 'tp'), may hold values from -0.09375 to 0.09375
- conv_x: float32 [4, 8192], P(None, 'tp'), may hold values from -2.5 to 2.5
- conv_bc: float32 [4, 256], replicated, may hold values from -2.5 to 2.5
- dt_bias: float32 [128], P('tp'), may hold values from -3 to 0
- decay_rate: float32 [128], P('tp'), may hold values from 6.1035155e-07 to 0.07
- d_skip: float32 [128], P('tp'), may hold values from 0.5 to 2
- norm_gain: float32 [8192], P('tp'), may hold values from 0.5 to 1.5
- initial_state: float32 [128, 64, 128], P('tp'), may hold values from -16 to 16
- steer: float32 [8192], P('tp'), may hold values from -6 to 6
Outputs:
- steered: bfloat16 [16384, 8192], P('seq', 'tp')
All inputs are finite; a program needn't handle non-finite values.
Results may differ from a plain program's by a relative error of at most 0.0055.
Values may be sent and summed in bfloat16 or wider, within the bound.
No kernel may reach another device: no remote copies, remote signals or barrier semaphores. Data moves between devices by JAX's collectives and lax.ppermute only.
A program may use at most 64 MiB of HBM per device.

v0:
```python
import jax
import jax.numpy as jnp
from jax import lax
from jax.sharding import PartitionSpec as P

N = 128
GROUP = 128
EPSILON = 1e-05


def passed_along(value, axis, steps):
    count = lax.axis_size(axis)
    first, last = (max(0, -steps), min(count, count - steps))
    return lax.ppermute(value, axis, [(source, source + steps) for source in range(first, last)])


def prefix(x, axis, combine, identity):
    count, mine = (lax.axis_size(axis), lax.axis_index(axis))
    everything = jax.tree.map(
        lambda part, kind: lax.all_gather(part.astype(kind), axis), x, (jnp.bfloat16, jnp.bfloat16)
    )
    start = jax.tree.map(
        lambda part, zero: jnp.broadcast_to(jnp.asarray(zero, part.dtype), part.shape), x, identity
    )

    def turn(k, before):
        reached = k < mine
        new = combine(
            before, jax.tree.map(lambda part, own: part[k].astype(own.dtype), everything, x)
        )
        return jax.tree.map(lambda a, b: jnp.where(reached, a, b), new, before)

    return lax.fori_loop(0, count, turn, start)


def convolve(extended, kernel):
    kernel_rows = kernel.shape[0]
    length = extended.shape[0] - kernel_rows + 1
    summed = kernel[0] * extended[0:length].astype(jnp.float32)
    for offset in range(1, kernel_rows):
        summed = summed + kernel[offset] * extended[offset : offset + length].astype(jnp.float32)
    return jax.nn.silu(summed).astype(jnp.bfloat16)


def block_update(carry_state, inputs):
    x_block, b_block, c_block, a_block, dt_block = inputs
    length = a_block.shape[0]
    cumulative = jnp.cumsum(a_block, axis=0)
    scores = jnp.dot(c_block, b_block.T, preferred_element_type=jnp.float32)
    causal = lax.broadcasted_iota(jnp.int32, (length, length), 0) >= lax.broadcasted_iota(
        jnp.int32, (length, length), 1
    )
    differ = cumulative[:, None, :] - cumulative[None, :, :]
    decays = jnp.where(causal[:, :, None], jnp.exp(jnp.where(causal[:, :, None], differ, 0.0)), 0.0)
    mixing = (scores[:, :, None] * decays * dt_block[None, :, :]).astype(jnp.bfloat16)
    inside = jnp.einsum("tsh,shp->thp", mixing, x_block, preferred_element_type=jnp.float32)
    carried_in = jnp.einsum(
        "tn,hpn->thp", c_block.astype(jnp.float32), carry_state, precision=lax.Precision.HIGHEST
    )
    outputs = inside + jnp.exp(cumulative)[:, :, None] * carried_in
    to_end = jnp.exp(cumulative[-1][None, :] - cumulative) * dt_block
    scaled = (x_block.astype(jnp.float32) * to_end[:, :, None]).astype(jnp.bfloat16)
    added_state = jnp.einsum("shp,sn->hpn", scaled, b_block, preferred_element_type=jnp.float32)
    return (jnp.exp(cumulative[-1])[:, None, None] * carry_state + added_state, outputs)


def combine_carry(earlier, later):
    return (earlier[0] * later[0], later[0][:, None, None] * earlier[1] + later[1])


def per_device(
    tokens,
    x_weight,
    bc_weight,
    dt_weight,
    conv_x,
    conv_bc,
    dt_bias,
    decay_rate,
    d_skip,
    norm_gain,
    initial_state,
    steer,
):
    features = lax.all_gather(tokens, "tp", axis=1, tiled=True)
    rim_rows = conv_x.shape[0] - 1
    local_tokens = features.shape[0]
    head_count = dt_weight.shape[1]
    channels = x_weight.shape[1]
    head_size = channels // head_count
    bc_panel = lax.all_gather(bc_weight, "tp", axis=1, tiled=True)
    x_sums = jnp.dot(
        features,
        lax.all_gather(x_weight, "seq", axis=0, tiled=True),
        preferred_element_type=jnp.float32,
    )
    bc_sums = jnp.dot(
        features,
        lax.all_gather(bc_panel, "seq", axis=0, tiled=True),
        preferred_element_type=jnp.float32,
    )
    dt_sums = jnp.dot(
        features,
        lax.all_gather(dt_weight, "seq", axis=0, tiled=True),
        preferred_element_type=jnp.float32,
    )
    x_pre = x_sums.astype(jnp.bfloat16)
    bc_pre = bc_sums.astype(jnp.bfloat16)
    joined = jnp.concatenate(
        [x_pre[local_tokens - rim_rows :], bc_pre[local_tokens - rim_rows :]], 1
    )
    arrived = passed_along(joined, "seq", 1)
    x_extended = jnp.concatenate([arrived[:, :channels], x_pre], 0)
    bc_extended = jnp.concatenate([arrived[:, channels:], bc_pre], 0)
    x_conv = convolve(x_extended, conv_x)
    bc_conv = convolve(bc_extended, conv_bc)
    b_values = bc_conv[:, :N]
    c_values = bc_conv[:, N:]
    step_size = jax.nn.softplus(dt_sums + dt_bias[None, :])
    log_decay = -step_size * decay_rate[None, :]
    blocks = local_tokens // GROUP
    x_heads = x_conv.reshape(local_tokens, head_count, head_size)
    inputs = (
        x_heads.reshape(blocks, GROUP, head_count, head_size),
        b_values.reshape(blocks, GROUP, N),
        c_values.reshape(blocks, GROUP, N),
        log_decay.reshape(blocks, GROUP, head_count),
        step_size.reshape(blocks, GROUP, head_count),
    )
    zero_state = jnp.zeros((head_count, head_size, N), jnp.float32)
    local_state, local_out = lax.scan(block_update, zero_state, inputs)
    running = jnp.cumsum(log_decay, axis=0)
    local_decay = jnp.exp(running[-1])
    identity = (
        jnp.ones((head_count,), jnp.float32),
        jnp.zeros((head_count, head_size, N), jnp.float32),
    )
    prefix_decay, prefix_state = prefix((local_decay, local_state), "seq", combine_carry, identity)
    entering = prefix_decay[:, None, None] * initial_state + prefix_state
    from_entering = jnp.einsum(
        "tn,hpn->thp", c_values.astype(jnp.float32), entering, precision=lax.Precision.HIGHEST
    )
    outputs = (
        local_out.reshape(local_tokens, head_count, head_size)
        + jnp.exp(running)[:, :, None] * from_entering
        + d_skip[None, :, None] * x_heads.astype(jnp.float32)
    )
    mean_square = jnp.mean(outputs * outputs, axis=-1, keepdims=True)
    normed = (outputs * lax.rsqrt(mean_square + EPSILON)).reshape(
        local_tokens, channels
    ) * norm_gain[None, :]
    partial_dot = jnp.sum(normed * steer[None, :], axis=1)
    total_dot = lax.psum(partial_dot, "tp")
    penalty = total_dot / jnp.sqrt(jnp.float32(channels * lax.axis_size("tp")))
    return (normed - penalty[:, None] * steer[None, :]).astype(jnp.bfloat16)


def solution(mesh):
    placed = (
        P("seq", "tp"),
        P("seq", "tp"),
        P("seq", "tp"),
        P("seq", "tp"),
        P(None, "tp"),
        P(),
        P("tp"),
        P("tp"),
        P("tp"),
        P("tp"),
        P("tp", None, None),
        P("tp"),
    )
    return jax.shard_map(
        per_device, mesh=mesh, in_specs=placed, out_specs=P("seq", "tp"), check_vma=False
    )
```

profile of v0, /device:TPU:1, one launch (start us, length us, event | category | flops | bytes accessed | tf_op | source)
XLA Modules:
  0.0 1208.3 jit_solution(8973249411349206538)
XLA Ops:
  7.3 21.4 %all_gather.28 = bf16[64,256]{0,1:T(8,128)(2,1)S(1)} all-gather(bf16[64,32]{0,1:T(8,128)(2,1)} %param.18), channel_id=1, replica_groups=mesh['seq'=64,'tp'=8] {'tp'}, dimensions={1}, use_global_device_ids=true | all-gather | bytes 36864 | tf_op jit(solution)/shard_map/all_gather | solution.py:91
  30.3 134.9 %all-gather.1 = bf16[64,64,16]{1,2,0:T(8,128)(2,1)S(1)} all-gather(bf16[1,64,16]{1,2,0:T(8,128)(2,1)} %bitcast.146), channel_id=1, replica_groups=mesh['seq'=64,'tp'=8] {'seq'}, dimensions={0}, use_global_device_ids=true | all-gather | bytes 133120 | tf_op jit(solution)/shard_map/all_gather | solution.py:104
  167.3 147.8 %all-gather.12.cloned.1.call-done = bf16[4096,256]{1,0:T(8,128)(2,1)} async-done(((bf16[64,256]{1,0:T(8,128)(2,1)}), bf16[4096,256]{1,0:T(8,128)(2,1)}) %all-gather.12.cloned.1.call-update) | async-done | bytes 2097168 | tf_op jit(solution)/shard_map/all_gather | solution.py:99
  315.1 2.9 convolution_convert_fusion.1
  318.1 328.3 %all-gather.10.cloned.1.call-done = bf16[4096,1024]{1,0:T(8,128)(2,1)} async-done(((bf16[64,1024]{1,0:T(8,128)(2,1)}), bf16[4096,1024]{1,0:T(8,128)(2,1)}) %all-gather.10.cloned.1.call-update) | async-done | bytes 8388624 | tf_op jit(solution)/shard_map/all_gather | solution.py:94
  646.4 5.7 convolution_convert_fusion
  652.2 1.9 collective-permute-start
  657.4 29.9 %while.29 = (s32[]{:T(128)}, f32[16,64,128]{2,1,0:T(8,128)S(1)}, f32[2,128,16,64]{1,0,3,2:T(2,128)}, f32[2,128,16]{2,1,0:T(8,128)S(1)}, bf16[2,128,16,64]{1,3,2,...) while((s32[]{:T(128)}, f32[16,64,128]{2,1,0:T(8,128)S(1)}, ...), condition=%wide.region_2.3_spmd.clone, body=%wide.region_0.2_spmd.clone.sunk | while | flops 275662848 | bytes 5196752 | solution.py:131
  659.0 13.0 %dynamic_update_slice.6 = f32[2,128,16,64]{1,0,3,2:T(2,128)} dynamic-update-slice(f32[2,128,16,64]{1,0,3,2:T(2,128)} %get-tuple-element.433, f32[1,128,16,64]{1,0,3,2:T(1,128)S(1)} %bitcast.133, s32[]{:T(128)} %get-tuple-element.431, s32[]{:T(128)} %constant.65.clone.1..sunk, s32[]{:T(128)} %constant.65.clone.1..sunk, s32[]{:T(128)} %constant.65.clone.1..sunk) | dynamic-update-slice | bytes 1048580 | tf_op jit(solution)/shard_map/while/body/jit(dynamic_update_index_in_dim)/dynamic_update_slice | solution.py:131
  674.0 13.0 %dynamic_update_slice.6 = f32[2,128,16,64]{1,0,3,2:T(2,128)} dynamic-update-slice(f32[2,128,16,64]{1,0,3,2:T(2,128)} %get-tuple-element.433, f32[1,128,16,64]{1,0,3,2:T(1,128)S(1)} %bitcast.133, s32[]{:T(128)} %get-tuple-element.431, s32[]{:T(128)} %constant.65.clone.1..sunk, s32[]{:T(128)} %constant.65.clone.1..sunk, s32[]{:T(128)} %constant.65.clone.1..sunk) | dynamic-update-slice | bytes 1048580 | tf_op jit(solution)/shard_map/while/body/jit(dynamic_update_index_in_dim)/dynamic_update_slice | solution.py:131
  689.4 133.3 %all-gather.2 = bf16[64,1,16]{2,1,0:T(2,128)(2,1)S(1)} all-gather(bf16[1,1,16]{2,1,0:T(2,128)(2,1)S(1)} %bitcast.151), channel_id=1, replica_groups=mesh['seq'=64,'tp'=8] {'seq'}, dimensions={0}, use_global_device_ids=true | all-gather | bytes 2080 | tf_op jit(solution)/shard_map/all_gather | solution.py:20
  823.0 2.1 reshape.112
  825.1 286.8 %all-gather.14.cloned.1.call-done = bf16[1024,64,128]{2,1,0:T(8,128)(2,1)} async-done(((bf16[16,64,128]{2,1,0:T(8,128)(2,1)}), bf16[1024,64,128]{2,1,0:T(8,128)(2,1)}) %all-gather.14.cloned.1.call-update) | async-done | bytes 16777232 | tf_op jit(solution)/shard_map/all_gather | solution.py:20
  1111.9 73.0 %while.30 = (s32[]{:T(128)}, f32[16]{0:T(128)S(1)}, f32[16,64,128]{2,1,0:T(8,128)S(1)}, s32[]{:T(128)}, bf16[64,16]{1,0:T(8,128)(2,1)S(1)}, /*index=5*/bf16[64,16,64,128]{3,2,1,0:T(8,128)(2,1)}, s32[]{:T(128)}, s32[]{:T(128)}) while((s32[]{:T(128)}, f32[16]{0:T(128)S(1)}, f32[16,64,128]{2,1,0:T(8,128)S(1)}, s32[]{:T(128)}, ...), condition=%wide.region_6.7_spmd.clone, body=%wide.region_5.6_spmd.clone.sunk | while | flops 655428 | bytes 1311123 | solution.py:33
  1111.9 1.1 fusion.85
  1113.1 1.1 fusion.85
  1114.2 1.1 fusion.85
  1115.4 1.1 fusion.85
  1116.5 1.1 fusion.85
  1117.7 1.1 fusion.85
  1118.8 1.1 fusion.85
  1119.9 1.1 fusion.85
  1121.1 1.1 fusion.85
  1122.2 1.1 fusion.85
  1123.4 1.1 fusion.85
  1124.5 1.1 fusion.85
  1125.6 1.1 fusion.85
  1126.8 1.1 fusion.85
  1127.9 1.1 fusion.85
  1129.1 1.1 fusion.85
  1130.2 1.1 fusion.85
  1131.3 1.1 fusion.85
  1132.5 1.1 fusion.85
  1133.6 1.1 fusion.85
  1134.8 1.1 fusion.85
  1135.9 1.1 fusion.85
  1137.0 1.1 fusion.85
  1138.2 1.1 fusion.85
  1139.3 1.1 fusion.85
  1140.4 1.1 fusion.85
  1141.6 1.1 fusion.85
  1142.7 1.1 fusion.85
  1143.9 1.1 fusion.85
  1145.0 1.1 fusion.85
  1146.1 1.1 fusion.85
  1148.4 1.1 fusion.85
  1151.8 1.1 fusion.85
  1153.0 1.1 fusion.85
  1155.3 1.1 fusion.85
  1156.4 1.1 fusion.85
  1158.7 1.1 fusion.85
  1159.8 1.1 fusion.85
  1162.1 1.1 fusion.85
  1163.2 1.1 fusion.85
  1166.7 1.1 fusion.85
  1170.1 1.1 fusion.85
  1173.5 1.1 fusion.85
  1174.6 1.1 fusion.85
  1176.9 1.1 fusion.85
  1178.0 1.1 fusion.85
  1180.3 1.1 fusion.85
  1181.5 1.1 fusion.85
  1183.7 1.1 fusion.85
  1186.3 14.5 %psum.7 = f32[256]{0:T(256)S(1)} all-reduce(f32[256]{0:T(256)S(1)} %get-tuple-element.306), channel_id=1, replica_groups=mesh['seq'=64,'tp'=8] {'tp'}, use_global_device_ids=true, to_apply=%region_9.10 | all-reduce | flops 256 | bytes 2048 | tf_op jit(solution)/shard_map/psum | solution.py:153
  (172 shorter events, 33.7 us)
Async XLA Ops:
  6.5 160.7 %all-gather.8.cloned.1.call-start = ((), (), s32[]{:S(2)}) async-start(), calls=%async_computation | async-start | bytes 2359296 | tf_op jit(solution)/shard_map/all_gather | solution.py:85
  7.3 307.9 %all-gather.12.cloned.1.call-start = ((), (), s32[]{:S(2)}) async-start(), calls=%async_computation.2 | async-start | bytes 2129920 | tf_op jit(solution)/shard_map/all_gather | solution.py:99
  29.5 616.9 %all-gather.10.cloned.1.call-start = ((), (), s32[]{:S(2)}) async-start(), calls=%async_computation.1 | async-start | bytes 8519680 | tf_op jit(solution)/shard_map/all_gather | solution.py:94
  30.2 1081.7 %all-gather.14.cloned.1.call-start = ((), (), s32[]{:S(2)}) async-start(), calls=%async_computation.3 | async-start | bytes 17039360 | tf_op jit(solution)/shard_map/all_gather | solution.py:20
  167.3 479.1 %copy-start = (bf16[256,4096]{1,0:T(8,128)(2,1)S(1)}, bf16[256,4096]{1,0:T(8,128)(2,1)}, u32[]{:S(2)}) copy-start(bf16[256,4096]{1,0:T(8,128)(2,1)} %all-gather.8.cloned.1.call-done) | copy-start | bytes 6291460
  318.1 336.0 %copy-start.4 = (f32[16]{0:T(128)S(1)}, f32[16]{0:T(128)}, u32[]{:S(2)}) copy-start(f32[16]{0:T(128)} %param.23) | copy-start | bytes 196
  318.1 336.0 %copy-start.6 = (f32[16]{0:T(128)S(1)}, f32[16]{0:T(128)}, u32[]{:S(2)}) copy-start(f32[16]{0:T(128)} %param.22) | copy-start | bytes 196
  652.2 2.8 collective-permute-start
  657.4 30.8 %copy-start.3 = (f32[1024]{0:T(1024)S(1)}, f32[1024]{0:T(1024)}, u32[]{:S(2)}) copy-start(f32[1024]{0:T(1024)} %param.25) | copy-start | bytes 12292
  657.4 30.8 %copy-start.2 = (f32[1024]{0:T(1024)S(1)}, f32[1024]{0:T(1024)}, u32[]{:S(2)}) copy-start(f32[1024]{0:T(1024)} %param.27) | copy-start | bytes 12292
  1111.9 73.0 %copy-start.1 = (f32[16,64,128]{2,1,0:T(8,128)S(1)}, f32[16,64,128]{2,1,0:T(8,128)}, u32[]{:S(2)}) copy-start(f32[16,64,128]{2,1,0:T(8,128)} %param.26) | copy-start | bytes 1572868
  1111.9 73.0 %copy-start.5 = (f32[16]{0:T(128)S(1)}, f32[16]{0:T(128)}, u32[]{:S(2)}) copy-start(f32[16]{0:T(128)} %param.24) | copy-start | bytes 196
Sparse Core Ops, SparseCore 0:
  9.5 44.7 all-gather.7
  56.3 258.7 all-gather.11
  317.2 329.1 all-gather.9
  688.3 423.5 all-gather.13
where the time goes:
time: 1210 us
  waiting for transfers between devices  764 us (63%)
  blocking collectives  304 us (25%)
  other arithmetic  75.7 us (6%)
  local copies, waits for them, and re-layouts  34.1 us (3%)
  between operations  13.4 us (1%)
  matrix products  12.8 us (1%)
    all_gather x1, waiting for transfers between devices, per_device(): lax.all_gather(x_weight, 'seq', axis=0, tiled=True)  328 us
    all_gather x1, waiting for transfers between devices, prefix(): lax.all_gather(part.astype(kind), axis)  287 us
    all_gather x1, waiting for transfers between devices, per_device(): lax.all_gather(bc_panel, 'seq', axis=0, tiled=True)  148 us
    all_gather x1, blocking collectives, per_device(): lax.all_gather(dt_weight, 'seq', axis=0, tiled=True)  135 us
    all_gather x1, blocking collectives, prefix(): lax.all_gather(part.astype(kind), axis)  133 us
    select_n x128, other arithmetic, turn(): return jax.tree.map(lambda a, b: jnp.where(reached, a, b), new, before)  71.3 us
    dynamic_update_slice x2, local copies, waits for them, and re-layouts, per_device(): local_state, local_out = lax.scan(block_update, zero_state, inputs)  26.1 us
  transfers between devices with their start and end apart: 5, of which 3 were waited for; matrix products, arithmetic and copies ran while one was open for 1% of the time, Pallas kernels for 0%

commit v1 on v0

--- a/solution.py
+++ b/solution.py
@@ -91,7 +91,9 @@
     bc_panel = lax.all_gather(bc_weight, "tp", axis=1, tiled=True)
     x_sums = jnp.dot(
         features,
-        lax.all_gather(x_weight, "seq", axis=0, tiled=True),
+        jnp.concatenate(
+            lax.all_to_all(jnp.stack([x_weight] * lax.axis_size("seq")), "seq", 0, 0), axis=0
+        ),
         preferred_element_type=jnp.float32,
     )
     bc_sums = jnp.dot(

time: 1210 us -> 1030 us (0.85)
  waiting for transfers between devices: 764 us -> 422 us
  blocking collectives: 304 us -> 441 us
  starting transfers between devices: 1.98 us -> 17.9 us
    all_gather x1 -> x0, waiting for transfers between devices: 328 us -> none  [per_device(): lax.all_gather(x_weight, 'seq', axis=0, tiled=True)]
    all_gather x1, blocking collectives: 21.4 us -> 158 us  [per_device(): bc_panel = lax.all_gather(bc_weight, 'tp', axis=1, tiled=True)]
    all_to_all x0 -> x1, starting transfers between devices: none -> 15.8 us  [per_device(): lax.all_to_all(jnp.stack([x_weight] * lax.axis_size('seq')), 'seq', 0, 0)]
    all_gather x1, waiting for transfers between devices: 148 us -> 134 us  [per_device(): lax.all_gather(bc_panel, 'seq', axis=0, tiled=True)]
  transfers between devices with their start and end apart: 5 -> 5, of which waited for: 3 -> 2; matrix products, arithmetic and copies ran while one was open for 1% -> 1% of each run, Pallas kernels for 0% -> 0%
where the time goes in v1:
time: 1030 us; the launch traced here: 1020 us
  blocking collectives  441 us (43%)
  waiting for transfers between devices  422 us (41%)
  other arithmetic  75.7 us (7%)
  local copies, waits for them, and re-layouts  37.6 us (4%)
  starting transfers between devices  17.9 us (2%)
  between operations  13.5 us (1%)
  matrix products  12.8 us (1%)
    all_gather x1, waiting for transfers between devices, prefix(): lax.all_gather(part.astype(kind), axis)  286 us
    all_gather x1, blocking collectives, per_device(): bc_panel = lax.all_gather(bc_weight, 'tp', axis=1, tiled=True)  158 us
    all_gather x1, blocking collectives, per_device(): lax.all_gather(dt_weight, 'seq', axis=0, tiled=True)  137 us
    all_gather x1, waiting for transfers between devices, per_device(): lax.all_gather(bc_panel, 'seq', axis=0, tiled=True)  134 us
    all_gather x1, blocking collectives, prefix(): lax.all_gather(part.astype(kind), axis)  132 us
    select_n x128, other arithmetic, turn(): return jax.tree.map(lambda a, b: jnp.where(reached, a, b), new, before)  71.3 us
    dynamic_update_slice x2, local copies, waits for them, and re-layouts, per_device(): local_state, local_out = lax.scan(block_update, zero_state, inputs)  26.1 us
  transfers between devices with their start and end apart: 5, of which 2 were waited for; matrix products, arithmetic and copies ran while one was open for 1% of the time, Pallas kernels for 0%

profile of v1, /device:TPU:1, one launch (start us, length us, event | category | flops | bytes accessed | tf_op | source)
XLA Modules:
  0.0 1022.0 jit_solution(7644363658215580892)
XLA Ops:
  6.5 5.2 stack.2
  11.8 15.8 %all-to-all-start = ((bf16[64,64,1024]{2,1,0:T(8,128)(2,1)}), bf16[64,64,1024]{2,1,0:T(8,128)(2,1)}, u32[]{:S(2)}, u32[]{:S(2)}) async-start(bf16[64,64,1024]{2,1,0:T(8,128)(2,1)} %stack.2), calls=%async_computation | async-start | bytes 16777216 | tf_op jit(solution)/shard_map/all_to_all | solution.py:95
  28.3 157.8 %all_gather.24 = bf16[64,256]{0,1:T(8,128)(2,1)S(1)} all-gather(bf16[64,32]{0,1:T(8,128)(2,1)S(1)} %copy-done.5), channel_id=1, replica_groups=mesh['seq'=64,'tp'=8] {'tp'}, dimensions={1}, use_global_device_ids=true | all-gather | bytes 36864 | tf_op jit(solution)/shard_map/all_gather | solution.py:91
  187.0 136.7 %all-gather.1 = bf16[64,64,16]{1,2,0:T(8,128)(2,1)S(1)} all-gather(bf16[1,64,16]{1,2,0:T(8,128)(2,1)S(1)} %bitcast.147), channel_id=1, replica_groups=mesh['seq'=64,'tp'=8] {'seq'}, dimensions={0}, use_global_device_ids=true | all-gather | bytes 133120 | tf_op jit(solution)/shard_map/all_gather | solution.py:106
  324.1 134.5 %all-gather.9.cloned.1.call-done = bf16[4096,256]{1,0:T(8,128)(2,1)} async-done(((bf16[64,256]{1,0:T(8,128)(2,1)}), bf16[4096,256]{1,0:T(8,128)(2,1)}) %all-gather.9.cloned.1.call-update) | async-done | bytes 2097168 | tf_op jit(solution)/shard_map/all_gather | solution.py:101
  458.6 2.9 convolution_convert_fusion.1
  461.6 5.7 convolution_convert_fusion
  467.3 2.0 collective-permute-start
  472.7 29.9 %while.29 = (s32[]{:T(128)}, f32[16,64,128]{2,1,0:T(8,128)S(1)}, f32[2,128,16,64]{1,0,3,2:T(2,128)}, f32[2,128,16]{2,1,0:T(8,128)S(1)}, bf16[2,128,16,64]{1,3,2,...) while((s32[]{:T(128)}, f32[16,64,128]{2,1,0:T(8,128)S(1)}, ...), condition=%wide.region_2.3_spmd.clone, body=%wide.region_0.2_spmd.clone.sunk | while | flops 275662848 | bytes 5196752 | solution.py:133
  474.3 13.1 %dynamic_update_slice.6 = f32[2,128,16,64]{1,0,3,2:T(2,128)} dynamic-update-slice(f32[2,128,16,64]{1,0,3,2:T(2,128)} %get-tuple-element.433, f32[1,128,16,64]{1,0,3,2:T(1,128)S(1)} %bitcast.134, s32[]{:T(128)} %get-tuple-element.431, s32[]{:T(128)} %constant.65.clone.1..sunk, s32[]{:T(128)} %constant.65.clone.1..sunk, s32[]{:T(128)} %constant.65.clone.1..sunk) | dynamic-update-slice | bytes 1048580 | tf_op jit(solution)/shard_map/while/body/jit(dynamic_update_index_in_dim)/dynamic_update_slice | solution.py:133
  489.3 13.1 %dynamic_update_slice.6 = f32[2,128,16,64]{1,0,3,2:T(2,128)} dynamic-update-slice(f32[2,128,16,64]{1,0,3,2:T(2,128)} %get-tuple-element.433, f32[1,128,16,64]{1,0,3,2:T(1,128)S(1)} %bitcast.134, s32[]{:T(128)} %get-tuple-element.431, s32[]{:T(128)} %constant.65.clone.1..sunk, s32[]{:T(128)} %constant.65.clone.1..sunk, s32[]{:T(128)} %constant.65.clone.1..sunk) | dynamic-update-slice | bytes 1048580 | tf_op jit(solution)/shard_map/while/body/jit(dynamic_update_index_in_dim)/dynamic_update_slice | solution.py:133
  504.7 132.2 %all-gather.2 = bf16[64,1,16]{2,1,0:T(2,128)(2,1)S(1)} all-gather(bf16[1,1,16]{2,1,0:T(2,128)(2,1)S(1)} %bitcast.152), channel_id=1, replica_groups=mesh['seq'=64,'tp'=8] {'seq'}, dimensions={0}, use_global_device_ids=true | all-gather | bytes 2080 | tf_op jit(solution)/shard_map/all_gather | solution.py:20
  637.3 2.1 reshape.118
  639.3 286.3 %all-gather.11.cloned.1.call-done = bf16[1024,64,128]{2,1,0:T(8,128)(2,1)} async-done(((bf16[16,64,128]{2,1,0:T(8,128)(2,1)}), bf16[1024,64,128]{2,1,0:T(8,128)(2,1)}) %all-gather.11.cloned.1.call-update) | async-done | bytes 16777232 | tf_op jit(solution)/shard_map/all_gather | solution.py:20
  925.6 73.0 %while.30 = (s32[]{:T(128)}, f32[16]{0:T(128)S(1)}, f32[16,64,128]{2,1,0:T(8,128)S(1)}, s32[]{:T(128)}, bf16[64,16]{1,0:T(8,128)(2,1)S(1)}, /*index=5*/bf16[64,16,64,128]{3,2,1,0:T(8,128)(2,1)}, s32[]{:T(128)}, s32[]{:T(128)}) while((s32[]{:T(128)}, f32[16]{0:T(128)S(1)}, f32[16,64,128]{2,1,0:T(8,128)S(1)}, s32[]{:T(128)}, ...), condition=%wide.region_6.7_spmd.clone, body=%wide.region_5.6_spmd.clone.sunk | while | flops 655428 | bytes 1311123 | solution.py:33
  925.7 1.1 fusion.85
  926.8 1.1 fusion.85
  928.0 1.1 fusion.85
  929.1 1.1 fusion.85
  930.3 1.1 fusion.85
  931.4 1.1 fusion.85
  932.5 1.1 fusion.85
  933.7 1.1 fusion.85
  934.8 1.1 fusion.85
  936.0 1.1 fusion.85
  937.1 1.1 fusion.85
  938.2 1.1 fusion.85
  939.4 1.1 fusion.85
  940.5 1.1 fusion.85
  941.7 1.1 fusion.85
  942.8 1.1 fusion.85
  943.9 1.1 fusion.85
  945.1 1.1 fusion.85
  946.2 1.1 fusion.85
  947.4 1.1 fusion.85
  948.5 1.1 fusion.85
  949.6 1.1 fusion.85
  950.8 1.1 fusion.85
  951.9 1.1 fusion.85
  953.0 1.1 fusion.85
  954.2 1.1 fusion.85
  955.3 1.1 fusion.85
  956.5 1.1 fusion.85
  957.6 1.1 fusion.85
  958.7 1.1 fusion.85
  961.0 1.1 fusion.85
  964.4 1.1 fusion.85
  967.9 1.1 fusion.85
  969.0 1.1 fusion.85
  971.3 1.1 fusion.85
  972.4 1.1 fusion.85
  974.7 1.1 fusion.85
  975.8 1.1 fusion.85
  978.1 1.1 fusion.85
  979.3 1.1 fusion.85
  982.7 1.1 fusion.85
  986.1 1.1 fusion.85
  989.5 1.1 fusion.85
  990.7 1.1 fusion.85
  992.9 1.1 fusion.85
  994.1 1.1 fusion.85
  996.3 1.1 fusion.85
  997.5 1.1 fusion.85
  1000.1 14.5 %psum.7 = f32[256]{0:T(256)S(1)} all-reduce(f32[256]{0:T(256)S(1)} %get-tuple-element.306), channel_id=1, replica_groups=mesh['seq'=64,'tp'=8] {'tp'}, use_global_device_ids=true, to_apply=%region_9.10 | all-reduce | flops 256 | bytes 2048 | tf_op jit(solution)/shard_map/psum | solution.py:155
  (180 shorter events, 32.4 us)
Async XLA Ops:
  11.7 16.6 %copy-start.5 = (bf16[64,32]{0,1:T(8,128)(2,1)S(1)}, bf16[64,32]{0,1:T(8,128)(2,1)}, u32[]{:S(2)}) copy-start(bf16[64,32]{0,1:T(8,128)(2,1)} %param.18) | copy-start | bytes 12292
  11.7 175.2 %copy-start.6 = (bf16[64,16]{0,1:T(8,128)(2,1)S(1)}, bf16[64,16]{0,1:T(8,128)(2,1)}, u32[]{:S(2)}) copy-start(bf16[64,16]{0,1:T(8,128)(2,1)} %param.19) | copy-start | bytes 6148
  11.7 312.3 %copy-start.7 = (f32[4,256]{1,0:T(4,128)S(1)}, f32[4,256]{1,0:T(4,128)}, u32[]{:S(2)}) copy-start(f32[4,256]{1,0:T(4,128)} %param.21) | copy-start | bytes 12292
  11.7 312.3 %copy-start.4 = (f32[4,1024]{1,0:T(4,128)S(1)}, f32[4,1024]{1,0:T(4,128)}, u32[]{:S(2)}) copy-start(f32[4,1024]{1,0:T(4,128)} %param.20) | copy-start | bytes 49156
  11.8 449.8 %all-to-all-start = ((bf16[64,64,1024]{2,1,0:T(8,128)(2,1)}), bf16[64,64,1024]{2,1,0:T(8,128)(2,1)}, u32[]{:S(2)}, u32[]{:S(2)}) async-start(bf16[64,64,1024]{2,1,0:T(8,128)(2,1)} %stack.2), calls=%async_computation | async-start | bytes 16777216 | tf_op jit(solution)/shard_map/all_to_all | solution.py:95
  27.5 296.6 %all-gather.7.cloned.1.call-start = ((), (), s32[]{:S(2)}) async-start(), calls=%async_computation.1 | async-start | bytes 2359296 | tf_op jit(solution)/shard_map/all_gather | solution.py:85
  28.2 430.3 %all-gather.9.cloned.1.call-start = ((), (), s32[]{:S(2)}) async-start(), calls=%async_computation.2 | async-start | bytes 2129920 | tf_op jit(solution)/shard_map/all_gather | solution.py:101
  186.9 738.8 %all-gather.11.cloned.1.call-start = ((), (), s32[]{:S(2)}) async-start(), calls=%async_computation.3 | async-start | bytes 17039360 | tf_op jit(solution)/shard_map/all_gather | solution.py:20
  324.1 137.5 %copy-start = (bf16[256,4096]{1,0:T(8,128)(2,1)S(1)}, bf16[256,4096]{1,0:T(8,128)(2,1)}, u32[]{:S(2)}) copy-start(bf16[256,4096]{1,0:T(8,128)(2,1)} %all-gather.7.cloned.1.call-done) | copy-start | bytes 6291460
  461.6 7.8 copy-start.8
  461.6 7.8 copy-start.10
  467.3 2.9 collective-permute-start
  472.7 30.8 %copy-start.3 = (f32[1024]{0:T(1024)S(1)}, f32[1024]{0:T(1024)}, u32[]{:S(2)}) copy-start(f32[1024]{0:T(1024)} %param.25) | copy-start | bytes 12292
  472.7 30.8 %copy-start.2 = (f32[1024]{0:T(1024)S(1)}, f32[1024]{0:T(1024)}, u32[]{:S(2)}) copy-start(f32[1024]{0:T(1024)} %param.27) | copy-start | bytes 12292
  925.6 73.0 %copy-start.1 = (f32[16,64,128]{2,1,0:T(8,128)S(1)}, f32[16,64,128]{2,1,0:T(8,128)}, u32[]{:S(2)}) copy-start(f32[16,64,128]{2,1,0:T(8,128)} %param.26) | copy-start | bytes 1572868
  925.6 73.0 %copy-start.9 = (f32[16]{0:T(128)S(1)}, f32[16]{0:T(128)}, u32[]{:S(2)}) copy-start(f32[16]{0:T(128)} %param.24) | copy-start | bytes 196
Sparse Core Ops, SparseCore 0:
  30.5 47.6 all-gather.6
  187.0 271.5 all-gather.8
  503.6 422.0 all-gather.10
